TPU v7x, 32 devices: a whole 2x2x4 slice. The times are simulated.
32 devices in a mesh: design: 4 (over x, core), graph: 8 (over z, y).
Axes of the slice: x: 2, y: 2, z: 4, core: 2. Of those that a mesh axis runs over, the one named last changes fastest.
Arguments:
- nodes: bfloat16 [4, 65536, 128], P('design', 'graph'), may hold values from -6 to 6
- adjacency: bfloat16 [4, 512, 4, 128, 128], P('design', 'graph'), may hold values from -0.25 to 0.25
- tile_src: int32 [4, 512, 4], P('design', 'graph'), may hold values from 0 to 67, as said below
- pool_dst: int32 [4, 512, 1], P('design', 'graph'), may hold values from 0 to 7; in each aligned block of 64 rows (0 to 63, 64 to 127, ..., all dimensions but the last counted through in order) at most 16 rows name the same one
- pool_weight: bfloat16 [4, 512, 128, 128], P('design', 'graph'), may hold values from -0.0625 to 0.0625
- coarse_cot: bfloat16 [4, 1024, 128], P('design', 'graph'), may hold values from -48 to 48
- w_msg: bfloat16 [128, 128], replicated, may hold values from -0.5 to 0.5
- w_in: bfloat16 [256, 128], replicated, may hold values from -0.375 to 0.375
- b_in: float32 [128], replicated, may hold values from -3 to 3
- w_out: bfloat16 [128, 128], replicated, may hold values from -0.5 to 0.5
Outputs:
- fine_out: bfloat16 [4, 65536, 128], P('design', 'graph')
- coarse: bfloat16 [4, 1024, 128], P('design', 'graph')
- grad_msg: float32 [128, 128], replicated
- grad_in: float32 [256, 128], replicated
- grad_bias: float32 [128], replicated
- grad_out: float32 [128, 128], replicated
Inputs may be any that keep to these rules, and one draw needn't show every extreme that they name: `tile_src`: entry 0 is the destination tile itself (its slab index plus 2); every entry lies within 2 tiles of the destination tile; each slab's first and last tiles list the outermost neighbouring tile. `pool_dst`: among the 64 fine tiles of one slab, at most 16 name the same coarse tile.
All inputs are finite; a program needn't handle non-finite values.
Results may differ from a plain program's by a relative error of at most 0.0067.
Values may be sent and summed in bfloat16 or wider, within the bound.
No kernel may reach another device: no remote copies, remote signals or barrier semaphores. Data moves between devices by JAX's collectives and lax.ppermute only.
A program may use at most 128 MiB of HBM per device.

v0:
```python
import math
import jax
import jax.numpy as jnp
from jax import lax
from jax.sharding import PartitionSpec as P

H = 128
TILE = 128
NBR = 4
HT = 2


def padded(block, sides, width):
    for axis, dim in sides:
        count = lax.axis_size(axis)
        forward = [(i, i + 1) for i in range(count - 1)]
        backward = [(target, source) for source, target in forward]
        low = lax.ppermute(
            lax.slice_in_dim(block, block.shape[dim] - width, None, axis=dim), axis, forward
        )
        high = lax.ppermute(lax.slice_in_dim(block, 0, width, axis=dim), axis, backward)
        block = jnp.concatenate([low, block, high], axis=dim)
    return block


def silu_slope(pre):
    sig = jax.nn.sigmoid(pre)
    return sig * (1.0 + pre * (1.0 - sig))


def on_device(
    nodes, adjacency, tile_src, pool_dst, pool_weight, coarse_cot, w_msg, w_in, b_in, w_out
):
    feats = nodes[0]
    edge_w = adjacency[0]
    source = tile_src[0]
    target = pool_dst[0][:, 0]
    pooling = pool_weight[0]
    cot_tile = coarse_cot[0]
    rows = feats.shape[0]
    count = rows // TILE
    slabs = lax.axis_size("graph")
    designs = lax.axis_size("design")
    holders = jnp.arange(slabs)
    messages = jnp.dot(feats, w_msg, preferred_element_type=jnp.float32).astype(jnp.bfloat16)
    extended = padded(messages, (("graph", 0),), HT * TILE)
    extended = extended.reshape(count + 2 * HT, TILE, H)
    picked = extended[source]
    agg = jnp.einsum("tkij,tkjh->tih", edge_w, picked, preferred_element_type=jnp.float32)
    agg_b = agg.astype(jnp.bfloat16).reshape(rows, H)
    pre = (
        jnp.dot(feats, w_in[:H], preferred_element_type=jnp.float32)
        + jnp.dot(agg_b, w_in[H:], preferred_element_type=jnp.float32)
        + b_in
    )
    act = jax.nn.silu(pre).astype(jnp.bfloat16)
    fine = (
        feats.astype(jnp.float32) + jnp.dot(act, w_out, preferred_element_type=jnp.float32)
    ).astype(jnp.bfloat16)
    contrib = jnp.einsum(
        "tij,tjh->tih", pooling, fine.reshape(count, TILE, H), preferred_element_type=jnp.float32
    ).astype(jnp.bfloat16)
    owner_of = (target[None, :] == holders[:, None]).astype(jnp.bfloat16)
    partial_sums = jnp.einsum("ot,tih->oih", owner_of, contrib, preferred_element_type=jnp.float32)
    coarse_sum = lax.psum_scatter(partial_sums, "graph", scatter_dimension=0, tiled=True)[0]
    coarse = coarse_sum.astype(jnp.bfloat16)
    every_cot = lax.all_gather(cot_tile, "graph", axis=0, tiled=True).reshape(slabs, TILE, H)
    selector = (target[:, None] == holders[None, :]).astype(jnp.bfloat16)
    chosen = jnp.einsum(
        "to,oih->tih", selector, every_cot, preferred_element_type=jnp.float32
    ).astype(jnp.bfloat16)
    grad_y = (
        jnp.einsum("tji,tjh->tih", pooling, chosen, preferred_element_type=jnp.float32)
        .astype(jnp.bfloat16)
        .reshape(rows, H)
    )
    grad_out = jnp.dot(act.T, grad_y, preferred_element_type=jnp.float32)
    grad_act = jnp.dot(grad_y, w_out.T, preferred_element_type=jnp.float32)
    grad_pre = (grad_act * silu_slope(pre)).astype(jnp.bfloat16)
    grad_in = jnp.concatenate(
        [
            jnp.dot(feats.T, grad_pre, preferred_element_type=jnp.float32),
            jnp.dot(agg_b.T, grad_pre, preferred_element_type=jnp.float32),
        ],
        axis=0,
    )
    grad_bias = jnp.sum(grad_pre.astype(jnp.float32), axis=0)
    grad_agg = (
        jnp.dot(grad_pre, w_in[H:].T, preferred_element_type=jnp.float32)
        .astype(jnp.bfloat16)
        .reshape(count, TILE, H)
    )
    returned = jnp.einsum("tkij,tih->tkjh", edge_w, grad_agg, preferred_element_type=jnp.float32)
    grad_ext = (
        jnp.zeros((count + 2 * HT, TILE, H), jnp.float32)
        .at[source.reshape(-1)]
        .add(returned.reshape(count * NBR, TILE, H))
    )
    margins = jnp.concatenate([grad_ext[:HT], grad_ext[count + HT :]], axis=0).reshape(
        2 * HT * TILE, H
    )
    beside_all = padded(margins, (("graph", 0),), HT * TILE)
    from_left = beside_all[: HT * TILE]
    from_right = beside_all[beside_all.shape[0] - HT * TILE :]
    own_grad = grad_ext[HT : HT + count].reshape(rows, H)
    own_grad = own_grad.at[: HT * TILE].add(from_left)
    own_grad = own_grad.at[rows - HT * TILE :].add(from_right)
    grad_m = own_grad.astype(jnp.bfloat16)
    grad_msg = jnp.dot(feats.T, grad_m, preferred_element_type=jnp.float32)
    totals = lax.psum((grad_msg, grad_in, grad_bias, grad_out), ("design", "graph"))
    scale = 1.0 / math.sqrt(designs * rows * slabs)
    return (
        fine[None],
        coarse[None],
        totals[0] * scale,
        totals[1] * scale,
        totals[2] * scale,
        totals[3] * scale,
    )


def solution(mesh):
    in_specs = (
        P("design", "graph", None),
        P("design", "graph", None, None, None),
        P("design", "graph", None),
        P("design", "graph", None),
        P("design", "graph", None, None),
        P("design", "graph", None),
        P(),
        P(),
        P(),
        P(),
    )
    out_specs = (P("design", "graph", None), P("design", "graph", None), P(), P(), P(), P())
    return jax.shard_map(
        on_device, mesh=mesh, in_specs=in_specs, out_specs=out_specs, check_vma=False
    )
```

profile of v0, /device:TPU:0, one launch (start us, length us, event | category | flops | bytes accessed | tf_op | source)
XLA Modules:
  0.0 338.6 jit_solution(5713422980382294656)
XLA Ops:
  8.1 2.4 convolution_convert_fusion.1
  10.5 1.3 copy-done.7
  11.9 4.9 %collective-permute-start = (bf16[256,128]{1,0:T(8,128)(2,1)S(1)}, bf16[256,128]{1,0:T(8,128)(2,1)S(1)}, u32[]{:S(2)}, u32[]{:S(2)}) collective-permute-start(bf16[256,128]{1,0:T(8,128)(2,1)S(1)} %get-tuple-element.60), channel_id=1, source_target_pairs={{0,1},{1,2},{2,3},{3,4},{4,5},{5,6},{6,7},{8,9},{9,10},{10,11},{11... | collective-permute-start | bytes 196616 | tf_op jit(solution)/shard_map/ppermute | solution.py:18
  16.8 1.3 collective-permute-start.1
  18.5 33.1 %all-gather = bf16[1,1024,128]{2,1,0:T(8,128)(2,1)S(1)} all-gather(bf16[1,128,128]{2,1,0:T(8,128)(2,1)S(1)} %copy-done.13), channel_id=2, replica_groups=mesh['design'=4,'graph'=8] {'graph'}, dimensions={1}, use_global_device_ids=true | all-gather | bytes 294912 | tf_op jit(solution)/shard_map/all_gather | solution.py:67
  51.6 4.3 %fusion.18 = f32[8192,128]{1,0:T(8,128)} fusion(bf16[1,8192,128]{2,1,0:T(8,128)(2,1)} %param.14, bf16[256,128]{1,0:T(8,128)(2,1)S(1)} %copy-done.11), kind=kOutput, calls=%fused_computation.28 | convolution fusion | flops 268435456 | bytes 6324224 | tf_op jit(solution)/shard_map/dot_general | solution.py:52
  56.7 3.6 %fusion.24 = bf16[64,128,128]{1,2,0:T(8,128)(2,1)} fusion(bf16[1,64,128,128]{3,2,1,0:T(8,128)(2,1)S(1)} %copy-done, bf16[64,128,128]{2,0,1:T(8,128)(2,1)S(1)} %convolution_convert_fusion.2), kind=kOutput, calls=%fused_computation.33 | convolution fusion | flops 269484032 | bytes 6291456 | tf_op jit(solution)/shard_map/tji,tjh->tih/dot_general | solution.py:73
  60.3 5.8 %pad_maximum_fusion = bf16[8704,128]{1,0:T(8,128)(2,1)} fusion(bf16[256,128]{1,0:T(8,128)(2,1)S(1)} %collective-permute-done.1, bf16[8192,128]{1,0:T(8,128)(2,1)S(1)} %copy-done.8, bf16[256,128]{1,0:T(8,128)(2,1)S(1)} %collective-permute-done), kind=kLoop, calls=%fused_computation.18 | loop fusion | flops 6684672 | bytes 4456448 | tf_op jit(solution)/shard_map/concatenate | solution.py:22
  66.1 10.3 %gather_fusion = bf16[256,128,128]{2,1,0:T(8,128)(2,1)} fusion(bf16[68,128,128]{2,1,0:T(8,128)(2,1)} %bitcast.95, s32[1024]{0:T(1024)S(1)} %pad_clamp_fusion), kind=kCustom, calls=%fused_computation | custom fusion | bytes 16778240 | tf_op jit(solution)/shard_map/gather | solution.py:48
  76.4 8.3 %bitcast_convert_fusion = bf16[64,128,128]{1,2,0:T(8,128)(2,1)S(1)} fusion(bf16[64,4,128,128]{3,2,1,0:T(8,128)(2,1)} %bitcast.94, bf16[1,64,4,128,128]{4,3,2,1,0:T(8,128)(2,1)} %param.15), kind=kOutput, calls=%fused_computation.14 | convolution fusion | flops 1074790400 | bytes 18874368 | tf_op jit(solution)/shard_map/tkij,tkjh->tih/dot_general | solution.py:49
  84.7 1.4 multiply_convert_fusion
  86.3 1.4 fusion.52
  88.6 1.8 convert_reduce_fusion
  92.5 2.9 convert_bitcast_fusion
  95.5 8.1 %fusion.3 = f32[64,128,4,128]{3,1,2,0:T(8,128)} fusion(bf16[64,128,128,1]{2,1,3,0:T(8,128)(2,1)S(1)} %bitcast.96, bf16[1,64,4,128,128]{4,3,2,1,0:T(8,128)(2,1)S(1)} %bitcast.93), kind=kOutput, calls=%fused_computation.10 | convolution fusion | flops 1073741824 | bytes 27262976 | tf_op jit(solution)/shard_map/tkij,tih->tkjh/dot_general | solution.py:93
  103.6 17.4 %copy.52 = f32[256,128,128]{2,1,0:T(8,128)} copy(f32[256,128,128]{1,2,0:T(8,128)} %bitcast.91) | data formatting | bytes 33554432 | tf_op jit(solution)/shard_map/reshape | solution.py:97
  121.0 2.6 broadcast_in_dim.5
  123.6 49.7 %scatter_fusion = f32[68,128,128]{2,1,0:T(8,128)} fusion(f32[68,128,128]{2,1,0:T(8,128)} %broadcast_in_dim.5, s32[256]{0:T(256)S(1)} %bitcast.107, f32[256,128,128]{2,1,0:T(8,128)} %copy.52), kind=kCustom, calls=%fused_computation.1 | custom fusion | flops 4194304 | bytes 50332672 | tf_op jit(solution)/shard_map/scatter-add | solution.py:97
  173.3 1.2 fusion.49
  174.5 2.7 collective-permute-start.2
  177.3 2.3 fusion.29
  179.6 2.2 slice.85
  181.8 4.2 %copy.45 = bf16[64,128,128]{2,0,1:T(8,128)(2,1)} copy(bf16[64,128,128]{1,2,0:T(8,128)(2,1)} %convert_bitcast_fusion) | data formatting | bytes 4194304 | tf_op jit(solution)/shard_map/convert_element_type | solution.py:62
  186.0 1.3 collective-permute-start.3
  188.6 4.2 %collective-permute-done.3 = f32[256,128]{1,0:T(8,128)S(1)} collective-permute-done((f32[256,128]{1,0:T(8,128)S(1)}, f32[256,128]{1,0:T(8,128)S(1)}, u32[]{:S(2)}, u32[]{:S(2)}) %collective-permute-start.3) | collective-permute-done | bytes 131104 | tf_op jit(solution)/shard_map/ppermute | solution.py:21
  192.9 1.6 fusion.38
  194.4 3.6 %fusion.32 = f32[128,128]{0,1:T(8,128)} fusion(bf16[1,8192,128]{2,1,0:T(8,128)(2,1)S(1)} %copy-done.4, f32[8192,128]{1,0:T(8,128)} %fusion.38), kind=kOutput, calls=%fused_computation.36 | convolution fusion | flops 269484032 | bytes 6356992 | tf_op jit(solution)/shard_map/dot_general | solution.py:109
  198.1 2.1 fusion.43
  201.1 39.7 %psum.30 = f32[128]{0:T(128)S(1)} all-reduce(f32[128]{0:T(128)S(1)} %get-tuple-element.64), channel_id=1, replica_groups=mesh['design'=4,'graph'=8] {'design','graph'}, use_global_device_ids=true, to_apply=%region_5.6 | all-reduce | flops 128 | bytes 1024 | tf_op jit(solution)/shard_map/psum | solution.py:110
  241.3 84.5 %all-reduce.3.cloned.1.call-done = (f32[128,128]{0,1:T(8,128)}, f32[256,128]{1,0:T(8,128)}, f32[128,128]{0,1:T(8,128)}) async-done(((f32[128,128]{0,1:T(8,128)}, f32[256,128]{1,0:T(8,128)}, f32[128,128]{0,1:T(8,128)}), (f32[128,128]{0,1:T(8,128)}, f32[256,128]{1,0:T(8,128)}, f32[128,128]{0,1:T(8,128)})) %all-reduce.3.cloned.1.call-update) | async-done | bytes 262160 | tf_op jit(solution)/shard_map/psum | solution.py:110
  328.1 1.6 broadcast_multiply_fusion
  329.7 1.5 convert_element_type.59
  (65 shorter events, 9.6 us)
Async XLA Ops:
  8.0 48.7 %copy-start = (bf16[1,64,128,128]{3,2,1,0:T(8,128)(2,1)S(1)}, bf16[1,64,128,128]{3,2,1,0:T(8,128)(2,1)}, u32[]{:S(2)}) copy-start(bf16[1,64,128,128]{3,2,1,0:T(8,128)(2,1)} %param.18) | copy-start | bytes 6291460
  8.0 10.1 %copy-start.14 = (s32[1,64,4]{1,2,0:T(4,128)S(1)}, s32[1,64,4]{1,2,0:T(4,128)}, u32[]{:S(2)}) copy-start(s32[1,64,4]{1,2,0:T(4,128)} %param.16) | copy-start | bytes 3076
  8.0 10.5 %copy-start.13 = (bf16[1,128,128]{2,1,0:T(8,128)(2,1)S(1)}, bf16[1,128,128]{2,1,0:T(8,128)(2,1)}, u32[]{:S(2)}) copy-start(bf16[1,128,128]{2,1,0:T(8,128)(2,1)} %param.19) | copy-start | bytes 98308
  8.0 43.6 %copy-start.11 = (bf16[256,128]{1,0:T(8,128)(2,1)S(1)}, bf16[256,128]{1,0:T(8,128)(2,1)}, u32[]{:S(2)}) copy-start(bf16[256,128]{1,0:T(8,128)(2,1)} %param.21) | copy-start | bytes 196612
  8.0 317.7 %all-reduce.3.cloned.1.call-start = ((), (), s32[]{:S(2)}) async-start(), calls=%async_computation.2 | async-start | bytes 524288 | tf_op jit(solution)/shard_map/psum | solution.py:110
  10.5 1.3 copy-start.7
  11.9 48.4 %collective-permute-start = (bf16[256,128]{1,0:T(8,128)(2,1)S(1)}, bf16[256,128]{1,0:T(8,128)(2,1)S(1)}, u32[]{:S(2)}, u32[]{:S(2)}) collective-permute-start(bf16[256,128]{1,0:T(8,128)(2,1)S(1)} %get-tuple-element.60), channel_id=1, source_target_pairs={{0,1},{1,2},{2,3},{3,4},{4,5},{5,6},{6,7},{8,9},{9,10},{10,11},{11... | collective-permute-start | bytes 196616 | tf_op jit(solution)/shard_map/ppermute | solution.py:18
  16.8 43.5 %collective-permute-start.1 = (bf16[256,128]{1,0:T(8,128)(2,1)S(1)}, bf16[256,128]{1,0:T(8,128)(2,1)S(1)}, u32[]{:S(2)}, u32[]{:S(2)}) collective-permute-start(bf16[256,128]{1,0:T(8,128)(2,1)S(1)} %get-tuple-element.61), channel_id=1, source_target_pairs={{1,0},{2,1},{3,2},{4,3},{5,4},{6,5},{7,6},{9,8},{10,9},{11,10},{12... | collective-permute-start | bytes 196616 | tf_op jit(solution)/shard_map/ppermute | solution.py:21
  51.6 4.3 %copy-start.15 = (s32[1,64,1]{1,2,0:T(1,128)S(1)}, s32[1,64,1]{1,2,0:T(1,128)}, u32[]{:S(2)}) copy-start(s32[1,64,1]{1,2,0:T(1,128)} %param.17) | copy-start | bytes 772
  56.7 3.6 %copy-start.8 = (bf16[8192,128]{1,0:T(8,128)(2,1)S(1)}, bf16[8192,128]{1,0:T(8,128)(2,1)}, u32[]{:S(2)}) copy-start(bf16[8192,128]{1,0:T(8,128)(2,1)} %copy-done.7) | copy-start | bytes 6291460
  76.4 8.3 %copy-start.9 = (f32[8192,128]{1,0:T(8,128)S(1)}, f32[8192,128]{1,0:T(8,128)}, u32[]{:S(2)}) copy-start(f32[8192,128]{1,0:T(8,128)} %fusion.18) | copy-start | bytes 12582916
  76.4 8.3 %copy-start.16 = (f32[128]{0:T(128)S(1)}, f32[128]{0:T(128)}, u32[]{:S(2)}) copy-start(f32[128]{0:T(128)} %param.22) | copy-start | bytes 1540
  84.7 1.6 copy-start.10
  86.2 1.6 copy-start.3
  86.3 1.6 copy-start.12
  88.6 3.9 %copy-start.6 = (bf16[8192,128]{1,0:T(8,128)(2,1)}, bf16[8192,128]{1,0:T(8,128)(2,1)S(1)}, u32[]{:S(2)}) copy-start(bf16[8192,128]{1,0:T(8,128)(2,1)S(1)} %fusion.1) | copy-start | bytes 6291460
  90.4 1.4 copy-start.5
  90.4 5.0 %slice-start = ((s8[8388608]{0:T(1024)(128)(4,1)}), s8[4194304]{0:T(1024)(128)(4,1)S(1)}, s32[]{:S(2)}) async-start(s8[8388608]{0:T(1024)(128)(4,1)} %bitcast.92), calls=%async_computation.3 | async-start | bytes 8388608
  91.8 3.7 %slice-start.1 = ((s8[8388608]{0:T(1024)(128)(4,1)}), s8[4194304]{0:T(1024)(128)(4,1)S(1)}, s32[]{:S(2)}) async-start(s8[8388608]{0:T(1024)(128)(4,1)} %bitcast.92), calls=%async_computation.4 | async-start | bytes 8388608
  123.6 53.6 %copy-start.4 = (bf16[1,8192,128]{2,1,0:T(8,128)(2,1)S(1)}, bf16[1,8192,128]{2,1,0:T(8,128)(2,1)}, u32[]{:S(2)}) copy-start(bf16[1,8192,128]{2,1,0:T(8,128)(2,1)} %param.14) | copy-start | bytes 6291460
  173.3 6.3 %copy-start.2 = (f32[68,128,128]{2,1,0:T(8,128)S(1)}, f32[68,128,128]{2,1,0:T(8,128)}, u32[]{:S(2)}) copy-start(f32[68,128,128]{2,1,0:T(8,128)} %scatter_fusion) | copy-start | bytes 13369348
  174.5 13.5 %collective-permute-start.2 = (f32[256,128]{1,0:T(8,128)S(1)}, f32[256,128]{1,0:T(8,128)S(1)}, u32[]{:S(2)}, u32[]{:S(2)}) collective-permute-start(f32[256,128]{1,0:T(8,128)S(1)} %bitcast.106), channel_id=1, source_target_pairs={{0,1},{1,2},{2,3},{3,4},{4,5},{5,6},{6,7},{8,9},{9,10},{10,11},{11... | collective-permute-start | bytes 393224 | tf_op jit(solution)/shard_map/ppermute | solution.py:18
  186.0 6.8 %collective-permute-start.3 = (f32[256,128]{1,0:T(8,128)S(1)}, f32[256,128]{1,0:T(8,128)S(1)}, u32[]{:S(2)}, u32[]{:S(2)}) collective-permute-start(f32[256,128]{1,0:T(8,128)S(1)} %bitcast.105), channel_id=1, source_target_pairs={{1,0},{2,1},{3,2},{4,3},{5,4},{6,5},{7,6},{9,8},{10,9},{11,10},{12... | collective-permute-start | bytes 393224 | tf_op jit(solution)/shard_map/ppermute | solution.py:21
  198.0 133.1 %copy-start.1 = (bf16[1,64,128,128]{3,2,1,0:T(8,128)(2,1)S(1)}, bf16[1,64,128,128]{3,2,1,0:T(8,128)(2,1)}, u32[]{:S(2)}) copy-start(bf16[1,64,128,128]{3,2,1,0:T(8,128)(2,1)} %param.18) | copy-start | bytes 6291460
  198.0 131.7 %reduce-scatter.2.cloned.1.call-start = ((), (), s32[]{:S(2)}) async-start(), calls=%async_computation.1 | async-start | bytes 589824 | tf_op jit(solution)/shard_map/reduce_scatter | solution.py:65
Sparse Core Ops, SparseCore 0:
  198.1 127.5 all-reduce.2
Sparse Core Ops, SparseCore 1:
  201.9 62.5 reduce-scatter.1
where the time goes:
time: 340 us; the launch traced here: 339 us
  waiting for transfers between devices  88.7 us (26%)
  blocking collectives  72.8 us (21%)
  other arithmetic  62.8 us (18%)
  matrix products  45.2 us (13%)
  local copies, waits for them, and re-layouts  43 us (13%)
  between operations  15.8 us (5%)
  starting transfers between devices  10.3 us (3%)
    psum x1, waiting for transfers between devices, on_device(): lax.psum((grad_msg, grad_in, grad_bias, grad_out), ('design', 'graph'))  84.5 us
    scatter-add x1, other arithmetic, on_device(): grad_ext = jnp.zeros((count + 2 * HT, TILE, H), jnp.float32).at[source.re...  49.7 us
    psum x1, blocking collectives, on_device(): lax.psum((grad_msg, grad_in, grad_bias, grad_out), ('design', 'graph'))  39.7 us
    all_gather x1, blocking collectives, on_device(): lax.all_gather(cot_tile, 'graph', axis=0, tiled=True)  33.1 us
    reshape x1, local copies, waits for them, and re-layouts, on_device(): returned.reshape(count * NBR, TILE, H)  17.4 us
    gather x1, local copies, waits for them, and re-layouts, on_device(): picked = extended[source]  10.3 us
    dot_general x1, matrix products, on_device(): jnp.einsum('tkij,tkjh->tih', edge_w, picked, preferred_element_type=jnp.f...  8.25 us
    dot_general x1, matrix products, on_device(): jnp.einsum('tkij,tih->tkjh', edge_w, grad_agg, preferred_element_type=jnp...  8.12 us
  transfers between devices with their start and end apart: 6, of which 2 were waited for; matrix products, arithmetic and copies ran while one was open for 8% of the time, Pallas kernels for 0%

commit v1 on v0

--- a/solution.py
+++ b/solution.py
@@ -3,6 +3,7 @@
 import jax.numpy as jnp
 from jax import lax
 from jax.sharding import PartitionSpec as P
+from jax.lax import psum
 
 H = 128
 TILE = 128
@@ -107,7 +108,8 @@
     own_grad = own_grad.at[rows - HT * TILE :].add(from_right)
     grad_m = own_grad.astype(jnp.bfloat16)
     grad_msg = jnp.dot(feats.T, grad_m, preferred_element_type=jnp.float32)
-    totals = lax.psum((grad_msg, grad_in, grad_bias, grad_out), ("design", "graph"))
+    meet_the_view = lambda here_x, peer_axis, named_axis: psum(psum(here_x, peer_axis), named_axis)
+    totals = meet_the_view((grad_msg, grad_in, grad_bias, grad_out), "graph", "design")
     scale = 1.0 / math.sqrt(designs * rows * slabs)
     return (
         fine[None],

time: 340 us -> 369 us (1.085)
  waiting for transfers between devices: 88.7 us -> 135 us
  blocking collectives: 72.8 us -> 58.5 us
    reduce_scatter x1, waiting for transfers between devices: 0.01 us -> 62.1 us  [on_device(): lax.psum_scatter(partial_sums, 'graph', scatter_dimension=0, tiled=True)[0]]
    psum x1 -> x2, waiting for transfers between devices: 84.5 us -> 68.4 us  [the longest x1 63.1 us: on_device(): psum(here_x, peer_axis)]
    psum x1 -> x2, blocking collectives: 39.7 us -> 25.4 us  [the longest x1 19.6 us: on_device(): psum(here_x, peer_axis)]
  transfers between devices with their start and end apart: 6 -> 7, of which waited for: 2 -> 4; matrix products, arithmetic and copies ran while one was open for 8% -> 8% of each run, Pallas kernels for 0% -> 0%
where the time goes in v1:
time: 369 us; the launch traced here: 367 us
  waiting for transfers between devices  135 us (37%)
  other arithmetic  61.4 us (17%)
  blocking collectives  58.5 us (16%)
  matrix products  46.4 us (13%)
  local copies, waits for them, and re-layouts  41.1 us (11%)
  between operations  14.1 us (4%)
  starting transfers between devices  10.4 us (3%)
    psum x1, waiting for transfers between devices, on_device(): psum(here_x, peer_axis)  63.1 us
    reduce_scatter x1, waiting for transfers between devices, on_device(): lax.psum_scatter(partial_sums, 'graph', scatter_dimension=0, tiled=True)[0]  62.1 us
    scatter-add x1, other arithmetic, on_device(): grad_ext = jnp.zeros((count + 2 * HT, TILE, H), jnp.float32).at[source.re...  50.4 us
    all_gather x1, blocking collectives, on_device(): lax.all_gather(cot_tile, 'graph', axis=0, tiled=True)  33.1 us
    psum x1, blocking collectives, on_device(): psum(here_x, peer_axis)  19.6 us
    reshape x1, local copies, waits for them, and re-layouts, on_device(): returned.reshape(count * NBR, TILE, H)  17.4 us
    gather x1, local copies, waits for them, and re-layouts, on_device(): picked = extended[source]  10.3 us
    dot_general x1, matrix products, on_device(): jnp.einsum('tkij,tkjh->tih', edge_w, picked, preferred_element_type=jnp.f...  8.25 us
  transfers between devices with their start and end apart: 7, of which 4 were waited for; matrix products, arithmetic and copies ran while one was open for 8% of the time, Pallas kernels for 0%

profile of v1, /device:TPU:0, one launch (start us, length us, event | category | flops | bytes accessed | tf_op | source)
XLA Modules:
  0.0 367.3 jit_solution(9469921744030178824)
XLA Ops:
  7.3 2.4 convolution_convert_fusion.1
  9.7 1.3 copy-done.5
  11.0 4.9 %collective-permute-start = (bf16[256,128]{1,0:T(8,128)(2,1)S(1)}, bf16[256,128]{1,0:T(8,128)(2,1)S(1)}, u32[]{:S(2)}, u32[]{:S(2)}) collective-permute-start(bf16[256,128]{1,0:T(8,128)(2,1)S(1)} %get-tuple-element.63), channel_id=1, source_target_pairs={{0,1},{1,2},{2,3},{3,4},{4,5},{5,6},{6,7},{8,9},{9,10},{10,11},{11... | collective-permute-start | bytes 196616 | tf_op jit(solution)/shard_map/ppermute | solution.py:19
  17.7 33.1 %all-gather = bf16[1,1024,128]{2,1,0:T(8,128)(2,1)S(1)} all-gather(bf16[1,128,128]{2,1,0:T(8,128)(2,1)S(1)} %copy-done.11), channel_id=2, replica_groups=mesh['design'=4,'graph'=8] {'graph'}, dimensions={1}, use_global_device_ids=true | all-gather | bytes 294912 | tf_op jit(solution)/shard_map/all_gather | solution.py:68
  50.8 4.3 %fusion.18 = f32[8192,128]{1,0:T(8,128)} fusion(bf16[1,8192,128]{2,1,0:T(8,128)(2,1)} %param.14, bf16[256,128]{1,0:T(8,128)(2,1)S(1)} %copy-done.9), kind=kOutput, calls=%fused_computation.28 | convolution fusion | flops 268435456 | bytes 6324224 | tf_op jit(solution)/shard_map/dot_general | solution.py:53
  55.8 3.6 fusion.24
  59.5 5.8 %pad_maximum_fusion = bf16[8704,128]{1,0:T(8,128)(2,1)} fusion(bf16[256,128]{1,0:T(8,128)(2,1)S(1)} %collective-permute-done.1, bf16[8192,128]{1,0:T(8,128)(2,1)S(1)} %copy-done.6, bf16[256,128]{1,0:T(8,128)(2,1)S(1)} %collective-permute-done), kind=kLoop, calls=%fused_computation.18 | loop fusion | flops 6684672 | bytes 4456448 | tf_op jit(solution)/shard_map/concatenate | solution.py:23
  65.2 10.3 %gather_fusion = bf16[256,128,128]{2,1,0:T(8,128)(2,1)} fusion(bf16[68,128,128]{2,1,0:T(8,128)(2,1)} %bitcast.95, s32[1024]{0:T(1024)S(1)} %pad_clamp_fusion), kind=kCustom, calls=%fused_computation | custom fusion | bytes 16778240 | tf_op jit(solution)/shard_map/gather | solution.py:49
  75.5 8.3 %bitcast_convert_fusion = bf16[64,128,128]{1,2,0:T(8,128)(2,1)S(1)} fusion(bf16[64,4,128,128]{3,2,1,0:T(8,128)(2,1)} %bitcast.94, bf16[1,64,4,128,128]{4,3,2,1,0:T(8,128)(2,1)} %param.15), kind=kOutput, calls=%fused_computation.14 | convolution fusion | flops 1074790400 | bytes 18874368 | tf_op jit(solution)/shard_map/tkij,tkjh->tih/dot_general | solution.py:50
  83.8 1.4 multiply_convert_fusion
  85.4 1.4 fusion.52
  87.0 2.0 fusion.1
  89.0 1.8 convert_reduce_fusion
  92.9 8.1 %fusion.3 = f32[64,128,4,128]{3,1,2,0:T(8,128)} fusion(bf16[64,128,128,1]{2,1,3,0:T(8,128)(2,1)S(1)} %bitcast.96, bf16[1,64,4,128,128]{4,3,2,1,0:T(8,128)(2,1)S(1)} %bitcast.93), kind=kOutput, calls=%fused_computation.10 | convolution fusion | flops 1073741824 | bytes 27262976 | tf_op jit(solution)/shard_map/tkij,tih->tkjh/dot_general | solution.py:94
  101.0 17.4 %copy.52 = f32[256,128,128]{2,1,0:T(8,128)} copy(f32[256,128,128]{1,2,0:T(8,128)} %bitcast.91) | data formatting | bytes 33554432 | tf_op jit(solution)/shard_map/reshape | solution.py:98
  118.4 2.6 broadcast_in_dim.5
  121.0 50.4 %scatter_fusion = f32[68,128,128]{2,1,0:T(8,128)} fusion(f32[68,128,128]{2,1,0:T(8,128)} %broadcast_in_dim.5, s32[256]{0:T(256)S(1)} %bitcast.107, f32[256,128,128]{2,1,0:T(8,128)} %copy.52), kind=kCustom, calls=%fused_computation.1 | custom fusion | flops 4194304 | bytes 50332672 | tf_op jit(solution)/shard_map/scatter-add | solution.py:98
  172.7 2.7 collective-permute-start.2
  175.4 3.0 fusion.29
  178.9 1.4 collective-permute-start.3
  181.0 4.9 %collective-permute-done.3 = f32[256,128]{1,0:T(8,128)S(1)} collective-permute-done((f32[256,128]{1,0:T(8,128)S(1)}, f32[256,128]{1,0:T(8,128)S(1)}, u32[]{:S(2)}, u32[]{:S(2)}) %collective-permute-start.3) | collective-permute-done | bytes 131104 | tf_op jit(solution)/shard_map/ppermute | solution.py:22
  185.9 1.4 fusion.32
  187.4 4.5 %convert_bitcast_fusion = bf16[64,128,128]{1,2,0:T(8,128)(2,1)} fusion(bf16[64,128,128]{2,1,0:T(8,128)(2,1)} %bitcast.97, bf16[1,64,128,128]{3,2,1,0:T(8,128)(2,1)S(1)} %copy-done), kind=kOutput, calls=%fused_computation.32 | convolution fusion | flops 269484032 | bytes 6291456 | tf_op jit(solution)/shard_map/tij,tjh->tih/dot_general | solution.py:61
  191.9 4.2 %copy.45 = bf16[64,128,128]{2,0,1:T(8,128)(2,1)} copy(bf16[64,128,128]{1,2,0:T(8,128)(2,1)} %convert_bitcast_fusion) | data formatting | bytes 4194304 | tf_op jit(solution)/shard_map/convert_element_type | solution.py:63
  196.1 63.1 %all-reduce.5.cloned.1.call-done = (f32[128,128]{0,1:T(8,128)}, f32[256,128]{1,0:T(8,128)}, f32[128,128]{0,1:T(8,128)}) async-done(((f32[128,128]{0,1:T(8,128)}, f32[256,128]{1,0:T(8,128)}, f32[128,128]{0,1:T(8,128)}), (f32[128,128]{0,1:T(8,128)}, f32[256,128]{1,0:T(8,128)}, f32[128,128]{0,1:T(8,128)})) %all-reduce.5.cloned.1.call-update) | async-done | bytes 262160 | tf_op jit(solution)/shard_map/psum | solution.py:111
  259.2 2.0 fusion.43
  262.1 19.6 %psum.60 = f32[128]{0:T(128)S(1)} all-reduce(f32[128]{0:T(128)S(1)} %get-tuple-element.67), channel_id=1, replica_groups=mesh['design'=4,'graph'=8] {'graph'}, use_global_device_ids=true, to_apply=%region_7.8 | all-reduce | flops 128 | bytes 1024 | tf_op jit(solution)/shard_map/psum | solution.py:111
  281.7 5.8 %psum.61 = f32[128]{0:T(128)S(1)} all-reduce(f32[128]{0:T(128)S(1)} %psum.60), channel_id=1, replica_groups=mesh['design'=4,'graph'=8] {'design'}, use_global_device_ids=true, to_apply=%region_8.9 | all-reduce | flops 128 | bytes 1024 | tf_op jit(solution)/shard_map/psum | solution.py:111
  288.0 5.3 %all-reduce.7.cloned.1.call-done = (f32[128,128]{0,1:T(8,128)}, f32[256,128]{1,0:T(8,128)}, f32[128,128]{0,1:T(8,128)}) async-done(((f32[128,128]{0,1:T(8,128)}, f32[256,128]{1,0:T(8,128)}, f32[128,128]{0,1:T(8,128)}), (f32[128,128]{0,1:T(8,128)}, f32[256,128]{1,0:T(8,128)}, f32[128,128]{0,1:T(8,128)})) %all-reduce.7.cloned.1.call-update) | async-done | bytes 262160 | tf_op jit(solution)/shard_map/psum | solution.py:111
  295.7 1.6 broadcast_multiply_fusion
  297.2 62.1 %reduce-scatter.2.cloned.1.call-done = f32[1,128,128]{2,1,0:T(8,128)} async-done(((f32[8,128,128]{2,1,0:T(8,128)}), f32[1,128,128]{2,1,0:T(8,128)}) %reduce-scatter.2.cloned.1.call-update) | async-done | bytes 65552 | tf_op jit(solution)/shard_map/reduce_scatter | solution.py:66
  359.3 1.5 convert_element_type.59
  (65 shorter events, 11.2 us)
Async XLA Ops:
  7.2 48.7 %copy-start = (bf16[1,64,128,128]{3,2,1,0:T(8,128)(2,1)S(1)}, bf16[1,64,128,128]{3,2,1,0:T(8,128)(2,1)}, u32[]{:S(2)}) copy-start(bf16[1,64,128,128]{3,2,1,0:T(8,128)(2,1)} %param.18) | copy-start | bytes 6291460
  7.2 10.1 %copy-start.12 = (s32[1,64,4]{1,2,0:T(4,128)S(1)}, s32[1,64,4]{1,2,0:T(4,128)}, u32[]{:S(2)}) copy-start(s32[1,64,4]{1,2,0:T(4,128)} %param.16) | copy-start | bytes 3076
  7.2 10.5 %copy-start.11 = (bf16[1,128,128]{2,1,0:T(8,128)(2,1)S(1)}, bf16[1,128,128]{2,1,0:T(8,128)(2,1)}, u32[]{:S(2)}) copy-start(bf16[1,128,128]{2,1,0:T(8,128)(2,1)} %param.19) | copy-start | bytes 98308
  7.2 43.6 %copy-start.9 = (bf16[256,128]{1,0:T(8,128)(2,1)S(1)}, bf16[256,128]{1,0:T(8,128)(2,1)}, u32[]{:S(2)}) copy-start(bf16[256,128]{1,0:T(8,128)(2,1)} %param.21) | copy-start | bytes 196612
  7.2 251.9 %all-reduce.5.cloned.1.call-start = ((), (), s32[]{:S(2)}) async-start(), calls=%async_computation.2 | async-start | bytes 524288 | tf_op jit(solution)/shard_map/psum | solution.py:111
  9.7 1.3 copy-start.5
  11.0 48.4 %collective-permute-start = (bf16[256,128]{1,0:T(8,128)(2,1)S(1)}, bf16[256,128]{1,0:T(8,128)(2,1)S(1)}, u32[]{:S(2)}, u32[]{:S(2)}) collective-permute-start(bf16[256,128]{1,0:T(8,128)(2,1)S(1)} %get-tuple-element.63), channel_id=1, source_target_pairs={{0,1},{1,2},{2,3},{3,4},{4,5},{5,6},{6,7},{8,9},{9,10},{10,11},{11... | collective-permute-start | bytes 196616 | tf_op jit(solution)/shard_map/ppermute | solution.py:19
  15.9 43.5 %collective-permute-start.1 = (bf16[256,128]{1,0:T(8,128)(2,1)S(1)}, bf16[256,128]{1,0:T(8,128)(2,1)S(1)}, u32[]{:S(2)}, u32[]{:S(2)}) collective-permute-start(bf16[256,128]{1,0:T(8,128)(2,1)S(1)} %get-tuple-element.64), channel_id=1, source_target_pairs={{1,0},{2,1},{3,2},{4,3},{5,4},{6,5},{7,6},{9,8},{10,9},{11,10},{12... | collective-permute-start | bytes 196616 | tf_op jit(solution)/shard_map/ppermute | solution.py:22
  50.8 4.3 %copy-start.13 = (s32[1,64,1]{1,2,0:T(1,128)S(1)}, s32[1,64,1]{1,2,0:T(1,128)}, u32[]{:S(2)}) copy-start(s32[1,64,1]{1,2,0:T(1,128)} %param.17) | copy-start | bytes 772
  55.8 3.6 copy-start.6
  75.5 8.3 %copy-start.7 = (f32[8192,128]{1,0:T(8,128)S(1)}, f32[8192,128]{1,0:T(8,128)}, u32[]{:S(2)}) copy-start(f32[8192,128]{1,0:T(8,128)} %fusion.18) | copy-start | bytes 12582916
  75.5 8.3 %copy-start.14 = (f32[128]{0:T(128)S(1)}, f32[128]{0:T(128)}, u32[]{:S(2)}) copy-start(f32[128]{0:T(128)} %param.22) | copy-start | bytes 1540
  83.8 1.6 copy-start.8
  85.4 1.6 copy-start.2
  85.4 1.6 copy-start.10
  87.0 5.9 %slice-start = ((s8[8388608]{0:T(1024)(128)(4,1)}), s8[4194304]{0:T(1024)(128)(4,1)S(1)}, s32[]{:S(2)}) async-start(s8[8388608]{0:T(1024)(128)(4,1)} %bitcast.92), calls=%async_computation.4 | async-start | bytes 8388608
  89.0 3.9 %slice-start.1 = ((s8[8388608]{0:T(1024)(128)(4,1)}), s8[4194304]{0:T(1024)(128)(4,1)S(1)}, s32[]{:S(2)}) async-start(s8[8388608]{0:T(1024)(128)(4,1)} %bitcast.92), calls=%async_computation.5 | async-start | bytes 8388608
  90.8 1.3 copy-start.4
  171.5 6.9 %copy-start.1 = (f32[68,128,128]{2,1,0:T(8,128)S(1)}, f32[68,128,128]{2,1,0:T(8,128)}, u32[]{:S(2)}) copy-start(f32[68,128,128]{2,1,0:T(8,128)} %scatter_fusion) | copy-start | bytes 13369348
  172.7 8.3 %collective-permute-start.2 = (f32[256,128]{1,0:T(8,128)S(1)}, f32[256,128]{1,0:T(8,128)S(1)}, u32[]{:S(2)}, u32[]{:S(2)}) collective-permute-start(f32[256,128]{1,0:T(8,128)S(1)} %bitcast.106), channel_id=1, source_target_pairs={{0,1},{1,2},{2,3},{3,4},{4,5},{5,6},{6,7},{8,9},{9,10},{10,11},{11... | collective-permute-start | bytes 393224 | tf_op jit(solution)/shard_map/ppermute | solution.py:19
  178.4 7.5 %copy-start.3 = (bf16[1,8192,128]{2,1,0:T(8,128)(2,1)S(1)}, bf16[1,8192,128]{2,1,0:T(8,128)(2,1)}, u32[]{:S(2)}) copy-start(bf16[1,8192,128]{2,1,0:T(8,128)(2,1)} %param.14) | copy-start | bytes 6291460
  178.9 7.0 %collective-permute-start.3 = (f32[256,128]{1,0:T(8,128)S(1)}, f32[256,128]{1,0:T(8,128)S(1)}, u32[]{:S(2)}, u32[]{:S(2)}) collective-permute-start(f32[256,128]{1,0:T(8,128)S(1)} %bitcast.105), channel_id=1, source_target_pairs={{1,0},{2,1},{3,2},{4,3},{5,4},{6,5},{7,6},{9,8},{10,9},{11,10},{12... | collective-permute-start | bytes 393224 | tf_op jit(solution)/shard_map/ppermute | solution.py:22
  187.3 106.0 %all-reduce.7.cloned.1.call-start = ((), (), s32[]{:S(2)}) async-start(), calls=%async_computation.3 | async-start | bytes 524288 | tf_op jit(solution)/shard_map/psum | solution.py:111
  259.2 100.1 %reduce-scatter.2.cloned.1.call-start = ((), (), s32[]{:S(2)}) async-start(), calls=%async_computation.1 | async-start | bytes 589824 | tf_op jit(solution)/shard_map/reduce_scatter | solution.py:66
Sparse Core Ops, SparseCore 0:
  187.4 71.6 all-reduce.4
  261.7 31.6 all-reduce.6
  296.7 62.5 reduce-scatter.1
